TPU v7x, 512 devices: a whole 4x8x8 slice. The times are simulated.
512 devices in a mesh: seq: 16 (over y, core), kv: 8 (over z), dp: 4 (over x).
Axes of the slice: x: 4, y: 8, z: 8, core: 2. Of those that a mesh axis runs over, the one named last changes fastest.
Arguments:
- queries: bfloat16 [65536, 2048], P(('dp', 'seq', 'kv')), parts along dimension 0, may hold values from -9 to 9
- keys: bfloat16 [65536, 512], P(('dp', 'seq', 'kv')), parts along dimension 0, may hold values from -4 to 4
- values: bfloat16 [65536, 512], P(('dp', 'seq', 'kv')), parts along dimension 0, may hold values from -6 to 6
- doc_ids: int32 [65536], P(('dp', 'seq', 'kv')), parts along dimension 0, may hold values from 0 to 7, never falling along the last dimension, each value on 1 to 4096 neighbouring positions
- beta: float32 [16], replicated, may hold values from -2 to 2
- lin_gain: float32 [2048], replicated, may hold values from 0.1 to 1.9
Outputs:
- mixed: float32 [65536, 2048], P(('dp', 'seq', 'kv')), parts along dimension 0
There are 4 independent parts, one for each index of `dp`. A program takes and returns all parts, laid end to end along the dimension named above; an argument that names none is the same for every part. Nothing has to cross between parts.
Inputs may be any that keep to these rules, and one draw needn't show every extreme that they name: `doc_ids`: document ids never fall along a packed sequence; each document holds 1 to 4096 tokens.
All inputs are finite; a program needn't handle non-finite values.
Results may differ from a plain program's by a relative error of at most 0.0012.
Values may be sent and summed in bfloat16 or wider, within the bound.
A program may use at most 64 MiB of HBM per device.

v0:
```python
import jax
import jax.numpy as jnp
from jax import lax
from jax.sharding import Mesh
from jax.sharding import PartitionSpec as P

HEADS = 16
KV_HEADS = 4
HEAD_DIM = 128
SEQ = ("seq_0", "seq_1")
DP_SEQ_KV = ("dp", "seq_0", "seq_1", "kv")


def in_one_piece(arrays, axis, dim, along):
    widths = [a.shape[along] for a in arrays]
    both = jnp.concatenate(arrays, axis=along)
    out = lax.all_gather(both, axis, axis=dim, tiled=True)
    return tuple(jnp.split(out, [sum(widths[:k]) for k in range(1, len(widths))], axis=along))


def nothing_yet(x, identity):
    return jax.tree.map(
        lambda part, zero: jnp.zeros_like(part) + jnp.asarray(zero, part.dtype), x, identity
    )


def all_in_one(x, axis):
    leaves = jax.tree.leaves(x)
    order = sorted(range(len(leaves)), key=lambda k: -leaves[k].size)
    width = (1, *leaves[order[0]].shape)[-1]
    lines = [
        jnp.pad(leaves[k].reshape(-1), (0, -leaves[k].size % width)).reshape(-1, width)
        for k in order
    ]
    both, at, found = (lax.all_gather(jnp.concatenate(lines), axis), 0, {})
    for k, line in zip(order, lines):
        section = both[:, at : at + len(line)].reshape(len(both), -1)
        found[k] = section[:, : leaves[k].size].reshape(-1, *leaves[k].shape)
        at += len(line)
    numbers = iter(range(len(leaves)))
    return jax.tree.map(lambda _: found[next(numbers)], x)


def collected_alike(x, axis):
    leaves, found = (jax.tree.leaves(x), {})
    for initial, a in enumerate(leaves):
        if initial not in found:
            alike = [k for k, b in enumerate(leaves) if b.dtype == a.dtype]
            got = (
                all_in_one([leaves[k] for k in alike], axis)
                if len(alike) > 1
                else [lax.all_gather(a, axis)]
            )
            for k, b in zip(alike, got):
                found[k] = b
    numbers = iter(range(len(leaves)))
    return jax.tree.map(lambda _: found[next(numbers)], x)


def prefix_by_axis(x, axes, combine, identity):
    before = start = nothing_yet(x, identity)
    so_far = x
    for axis in reversed(axes):
        size, here = (lax.axis_size(axis), lax.axis_index(axis))
        pieces = collected_alike(so_far, axis)
        inside, so_far = (start, start)
        for k in range(size):
            passed = k < here
            so_far = combine(so_far, jax.tree.map(lambda part: part[k], pieces))
            inside = jax.tree.map(lambda new, old: jnp.where(passed, new, old), so_far, inside)
        before = combine(inside, before)
    return before


def join_states(earlier, later):
    state_early, first_early, last_early = earlier
    state_late, first_late, last_late = later
    empty_late = first_late < 0
    joined = (first_late == last_late) & (last_early == first_late)
    merged = state_late + jnp.where(joined, state_early, jnp.zeros_like(state_early))
    combined = jnp.where(empty_late, state_early, merged)
    first_doc = jnp.where(first_early < 0, first_late, first_early)
    last_doc = jnp.where(empty_late, last_early, last_late)
    return (combined, first_doc, last_doc)


def tail_merge(one_side, other_side):
    state_one, first_one, last_one = one_side
    state_other, first_other, last_other = other_side
    top_doc = jnp.maximum(last_one, last_other)
    state_sum = jnp.where(last_one == top_doc, state_one, jnp.zeros_like(state_one))
    state_sum = state_sum + jnp.where(
        last_other == top_doc, state_other, jnp.zeros_like(state_other)
    )
    return (state_sum, jnp.minimum(first_one, first_other), top_doc)


def tail_state(key_rows, value_rows, doc_rows, target_doc):
    count = key_rows.shape[0]
    key_heads = key_rows.reshape(count, KV_HEADS, HEAD_DIM)
    value_heads = value_rows.reshape(count, KV_HEADS, HEAD_DIM)
    live = doc_rows == target_doc
    masked = jnp.where(live[:, None, None], key_heads, jnp.zeros_like(key_heads))
    return jnp.einsum("rgd,rge->gde", masked, value_heads, preferred_element_type=jnp.float32)


def attend_block(
    carry, query_heads, query_pos, query_doc, key_rows, value_rows, key_doc, key_start
):
    running_max, running_sum, accumulated = carry
    key_count = key_rows.shape[0]
    key_heads = key_rows.reshape(key_count, KV_HEADS, HEAD_DIM)
    value_heads = value_rows.reshape(key_count, KV_HEADS, HEAD_DIM)
    scores = jnp.einsum(
        "rgqd,kgd->gqrk", query_heads, key_heads, preferred_element_type=jnp.float32
    )
    scores = scores / jnp.sqrt(jnp.float32(HEAD_DIM))
    key_pos = key_start + jnp.arange(key_count, dtype=jnp.int32)
    allowed = (key_pos[None, :] <= query_pos[:, None]) & (key_doc[None, :] == query_doc[:, None])
    masked = jnp.where(allowed, scores, jnp.float32(-1e30))
    new_max = jnp.maximum(running_max, jnp.max(masked, axis=-1))
    factor = jnp.exp(running_max - new_max)
    weights = jnp.where(allowed, jnp.exp(masked - new_max[..., None]), jnp.float32(0.0))
    new_sum = running_sum * factor + jnp.sum(weights, axis=-1)
    product = jnp.einsum(
        "gqrk,kge->gqre",
        weights.astype(jnp.bfloat16),
        value_heads,
        preferred_element_type=jnp.float32,
    )
    new_accum = accumulated * factor[..., None] + product
    return (new_max, new_sum, new_accum)


def on_device(queries, keys, values, doc_ids, beta, lin_gain):
    row_count = queries.shape[0]
    groups = HEADS // KV_HEADS
    query_heads = queries.reshape(row_count, KV_HEADS, groups, HEAD_DIM)
    position = lax.axis_index("kv") * row_count
    query_pos = position + jnp.arange(row_count, dtype=jnp.int32)
    last_query = position + row_count - 1
    initial = (
        jnp.full((KV_HEADS, groups, row_count), -1e30, jnp.float32),
        jnp.zeros((KV_HEADS, groups, row_count), jnp.float32),
        jnp.zeros((KV_HEADS, groups, row_count, HEAD_DIM), jnp.float32),
    )
    empty_tail = (
        jnp.zeros((KV_HEADS, HEAD_DIM, HEAD_DIM), jnp.float32),
        jnp.array(2**30, jnp.int32),
        jnp.array(-1, jnp.int32),
    )
    key_piece, value_piece, doc_piece = (
        *in_one_piece((keys, values), "kv", 0, 1),
        lax.all_gather(doc_ids, "kv", axis=0, tiled=True),
    )
    blocks = key_piece.shape[0] // row_count

    def one_block(state, item):
        soft_state, tail_now = state
        key_block, value_block, doc_block, number = item
        block_start = number * row_count
        soft_next = lax.cond(
            block_start <= last_query,
            lambda inner: attend_block(
                inner,
                query_heads,
                query_pos,
                doc_ids,
                key_block,
                value_block,
                doc_block,
                block_start,
            ),
            lambda inner: inner,
            soft_state,
        )
        block_tail = (
            tail_state(key_block, value_block, doc_block, doc_block[-1]),
            doc_block[0],
            doc_block[-1],
        )
        tail_now = tail_merge(tail_now, block_tail)
        return ((soft_next, tail_now), None)

    stacked = (
        key_piece.reshape(blocks, row_count, -1),
        value_piece.reshape(blocks, row_count, -1),
        doc_piece.reshape(blocks, row_count),
        jnp.arange(blocks, dtype=jnp.int32),
    )
    result, _ = lax.scan(one_block, (initial, empty_tail), stacked)
    running, segment_tail = result
    running_max, running_sum, accumulated = running
    soft_out = jnp.transpose(accumulated / running_sum[..., None], (2, 0, 1, 3))
    identity = (
        jnp.zeros((KV_HEADS, HEAD_DIM, HEAD_DIM), jnp.float32),
        jnp.array(-1, jnp.int32),
        jnp.array(-1, jnp.int32),
    )
    memory = prefix_by_axis(segment_tail, SEQ, join_states, identity)
    memory_state, memory_first, memory_last = memory
    query_float = query_heads.astype(jnp.float32)
    recalled = jnp.einsum(
        "rgqd,gde->rgqe", query_float, memory_state, precision=lax.Precision.HIGHEST
    )
    recalled = jnp.where((doc_ids == memory_last)[:, None, None, None], recalled, jnp.float32(0.0))
    mean_square = jnp.mean(recalled * recalled, axis=-1, keepdims=True)
    normed = (
        recalled * lax.rsqrt(mean_square + 1e-06) * lin_gain.reshape(KV_HEADS, groups, HEAD_DIM)
    )
    mixing = jax.nn.sigmoid(beta).reshape(KV_HEADS, groups)[None, :, :, None]
    mixed = mixing * normed + (1.0 - mixing) * soft_out
    return mixed.reshape(row_count, HEADS * HEAD_DIM).astype(jnp.float32)


def solution(mesh):
    split = Mesh(
        mesh.devices.reshape(8, 2, mesh.shape["kv"], mesh.shape["dp"]),
        ("seq_0", "seq_1", "kv", "dp"),
    )
    in_specs = (P(DP_SEQ_KV, None), P(DP_SEQ_KV, None), P(DP_SEQ_KV, None), P(DP_SEQ_KV), P(), P())
    out_specs = P(DP_SEQ_KV, None)
    return jax.shard_map(
        on_device, mesh=split, in_specs=in_specs, out_specs=out_specs, check_vma=False
    )
```

profile of v0, /device:TPU:2, one launch (start us, length us, event | category | flops | bytes accessed | tf_op | source)
XLA Modules:
  0.0 181.8 jit_solution(15142142390558384804)
XLA Ops:
  6.5 1.7 pad_maximum_fusion
  8.3 1.3 copy.45
  10.0 1.3 dynamic-slice
  11.9 22.2 %all-gather.3 = s32[8,1,128]{2,1,0:T(1,128)S(1)} all-gather(s32[1,1,128]{2,1,0:T(1,128)S(1)} %bitcast.210), channel_id=1, replica_groups=mesh['seq_0'=8,'seq_1'=2,'kv'=8,'dp'=4] {'kv'}, dimensions={0}, use_global_device_ids=true | all-gather | bytes 4608 | tf_op jit(solution)/shard_map/all_gather | solution.py:154
  34.1 24.7 %all-gather.7.cloned.1.call-done = bf16[1024,1024]{1,0:T(8,128)(2,1)} async-done(((bf16[128,1024]{1,0:T(8,128)(2,1)}), bf16[1024,1024]{1,0:T(8,128)(2,1)}) %all-gather.7.cloned.1.call-update) | async-done | bytes 2097168 | tf_op jit(solution)/shard_map/all_gather | solution.py:17
  58.8 2.6 %fusion.103 = (bf16[1024,512]{1,0:T(8,128)(2,1)S(1)}, bf16[1024,512]{1,0:T(8,128)(2,1)}) fusion(bf16[1024,1024]{1,0:T(8,128)(2,1)} %all-gather.7.cloned.1.call-done), kind=kLoop, calls=%fused_computation.128 | loop fusion | bytes 4194304 | tf_op jit(solution)/shard_map/split | solution.py:18
  61.5 48.8 %while.21 = (s32[]{:T(128)}, f32[4,4,128]{2,1,0:T(4,128)S(1)}, f32[4,4,128]{2,1,0:T(4,128)S(1)}, f32[4,4,128,128]{3,2,1,0:T(8,128)S(1)}, f32[4,128,128]{2,1,0:T(...) while((s32[]{:T(128)}, f32[4,4,128]{2,1,0:T(4,128)S(1)}, ...), condition=%wide.region_5.6_spmd.clone, body=%wide.region_0.5_spmd.clone.sunk | while | flops 154259840 | bytes 8067273 | solution.py:191
  62.8 0.9 constant_dynamic-slice_fusion.6
  64.0 1.5 conditional.3
  70.2 0.9 constant_dynamic-slice_fusion.6
  76.1 0.9 constant_dynamic-slice_fusion.6
  82.0 0.9 constant_dynamic-slice_fusion.6
  87.9 0.9 constant_dynamic-slice_fusion.6
  93.8 0.9 constant_dynamic-slice_fusion.6
  99.8 0.9 constant_dynamic-slice_fusion.6
  105.7 0.9 constant_dynamic-slice_fusion.6
  110.5 2.3 %all-gather.2 = f32[8,128,128]{2,1,0:T(8,128)S(1)} all-gather(f32[4,128,128]{2,1,0:T(8,128)S(1)} %get-tuple-element.130), channel_id=4, replica_groups=mesh['seq_0'=8,'seq_1'=2,'kv'=8,'dp'=4] {'seq_1'}, dimensions={0}, use_global_device_ids=true | all-gather | bytes 786432 | tf_op jit(solution)/shard_map/all_gather | solution.py:52
  112.8 1.8 all-reduce
  119.2 0.7 fusion.34
  120.0 1.2 dynamic-slice.1
  124.9 13.5 %all-reduce.1 = s32[16]{0:T(128)S(1)} all-reduce(s32[16]{0:T(128)S(1)} %fusion.99), channel_id=3, replica_groups=mesh['seq_0'=8,'seq_1'=2,'kv'=8,'dp'=4] {'seq_0'}, use_global_device_ids=true, to_apply=%add.1 | all-reduce | flops 16 | bytes 128
  161.4 9.1 %all-gather.9.cloned.1.call-done = f32[8,4,128,128]{3,2,1,0:T(8,128)} async-done(((f32[1,4,128,128]{3,2,1,0:T(8,128)}), f32[8,4,128,128]{3,2,1,0:T(8,128)}) %all-gather.9.cloned.1.call-update) | async-done | bytes 2097168 | tf_op jit(solution)/shard_map/all_gather | solution.py:52
  170.5 2.6 %multiply_reduce_fusion = (f32[128,4,4]{0,2,1:T(4,128)S(1)}, f32[128,4,4,128]{0,3,2,1:T(8,128)S(1)}) fusion(bf16[128,4,4,128]{0,3,2,1:T(8,128)(2,1)S(1)} %bitcast.203, f32[8,4,128,128]{3,2,1,0:T(8,128)} %all-gather.9.cloned.1.call-done, f32[8,128,128]{2,1,0:T(8,128)S(1)} %all-gather.2, pred[]{:T(512)S(6)} %lt.43, pred[]{:T(512)S(6)} %and.43, pred[]{:T(512)S(6)} %gt.31, ...), kind=kOutput, calls=%fused_computation.31 | convolution fusion | flops 405993472 | bytes 4202654 | tf_op jit(solution)/shard_map/rgqd,gde->rgqe/dot_general | solution.py:203
  173.6 1.3 copy.52
  (114 shorter events, 23.5 us)
Async XLA Ops:
  6.5 5.3 %copy-start.2 = (s32[128]{0:T(128)S(1)}, s32[128]{0:T(128)}, u32[]{:S(2)}) copy-start(s32[128]{0:T(128)} %param.13) | copy-start | bytes 1540
  6.5 52.2 %all-gather.7.cloned.1.call-start = ((), (), s32[]{:S(2)}) async-start(), calls=%async_computation | async-start | bytes 2359296 | tf_op jit(solution)/shard_map/all_gather | solution.py:17
  8.3 162.2 %all-gather.9.cloned.1.call-start = ((), (), s32[]{:S(2)}) async-start(), calls=%async_computation.1 | async-start | bytes 2359296 | tf_op jit(solution)/shard_map/all_gather | solution.py:52
  9.7 51.8 %copy-start = (bf16[128,2048]{0,1:T(8,128)(2,1)}, bf16[128,2048]{0,1:T(8,128)(2,1)S(1)}, u32[]{:S(2)}) copy-start(bf16[128,2048]{0,1:T(8,128)(2,1)S(1)} %copy.45) | copy-start | bytes 1572868
  61.5 60.2 %copy-start.4 = (f32[16]{0:T(128)S(1)}, f32[16]{0:T(128)}, u32[]{:S(2)}) copy-start(f32[16]{0:T(128)} %param.14) | copy-start | bytes 196
  110.5 60.0 %copy-start.1 = (bf16[128,2048]{0,1:T(8,128)(2,1)S(1)}, bf16[128,2048]{0,1:T(8,128)(2,1)}, u32[]{:S(2)}) copy-start(bf16[128,2048]{0,1:T(8,128)(2,1)} %copy-done) | copy-start | bytes 1572868
  161.3 11.8 %copy-start.3 = (f32[2048]{0:T(1024)S(1)}, f32[2048]{0:T(1024)}, u32[]{:S(2)}) copy-start(f32[2048]{0:T(1024)} %param.15) | copy-start | bytes 24580
Sparse Core Ops, SparseCore 0:
  9.4 49.2 all-gather.6
  120.1 50.3 all-gather.8
where the time goes:
time: 183 us; the launch traced here: 182 us
  between operations  43.2 us (24%)
  blocking collectives  39.9 us (22%)
  waiting for transfers between devices  33.8 us (18%)
  local copies, waits for them, and re-layouts  29.4 us (16%)
  loops' own time  21.2 us (12%)
  other arithmetic  8.77 us (5%)
  matrix products  5.49 us (3%)
    all_gather x1, waiting for transfers between devices, in_one_piece(): out = lax.all_gather(both, axis, axis=dim, tiled=True)  24.7 us
    all_gather x1, blocking collectives, on_device(): lax.all_gather(doc_ids, 'kv', axis=0, tiled=True)  22.2 us
    another operation x1, loops' own time, on_device(): result, _ = lax.scan(one_block, (initial, empty_tail), stacked)  21 us
    unnamed x2, blocking collectives  15.3 us
    dynamic_slice x40, local copies, waits for them, and re-layouts, on_device(): result, _ = lax.scan(one_block, (initial, empty_tail), stacked)  14.4 us
    all_gather x1, waiting for transfers between devices, collected_alike(): lax.all_gather(a, axis)  9.14 us
    eq x8, other arithmetic, tail_state(): live = doc_rows == target_doc  5.13 us
    slice x8, local copies, waits for them, and re-layouts, one_block(): doc_block[0]  4.86 us
  transfers between devices with their start and end apart: 2, of which 2 were waited for; matrix products, arithmetic and copies ran while one was open for 3% of the time, Pallas kernels for 0%

commit v1 on v0

--- a/solution.py
+++ b/solution.py
@@ -3,6 +3,7 @@
 from jax import lax
 from jax.sharding import Mesh
 from jax.sharding import PartitionSpec as P
+from jax.lax import all_to_all, axis_size
 
 HEADS = 16
 KV_HEADS = 4
@@ -133,6 +134,15 @@
 
 
 def on_device(queries, keys, values, doc_ids, beta, lin_gain):
+
+    def attach_ladders(incoming_x, shard_axis):
+        crops = []
+        for _ in range(axis_size(shard_axis)):
+            crops.append(incoming_x)
+        n_now = jnp.stack(crops)
+        left_arr = all_to_all(n_now, shard_axis, 0, 0)
+        return jnp.concatenate(left_arr, axis=0)
+
     row_count = queries.shape[0]
     groups = HEADS // KV_HEADS
     query_heads = queries.reshape(row_count, KV_HEADS, groups, HEAD_DIM)
@@ -151,7 +161,7 @@
     )
     key_piece, value_piece, doc_piece = (
         *in_one_piece((keys, values), "kv", 0, 1),
-        lax.all_gather(doc_ids, "kv", axis=0, tiled=True),
+        attach_ladders(doc_ids, "kv"),
     )
     blocks = key_piece.shape[0] // row_count
 

time: 183 us -> 183 us (level)
  blocking collectives: 39.9 us -> 17.6 us
  waiting for transfers between devices: 33.8 us -> 44.3 us
  starting transfers between devices: 0.04 us -> 10.4 us
  local copies, waits for them, and re-layouts: 29.4 us -> 31.4 us
    all_gather x1 -> x0, blocking collectives: 22.2 us -> none  [on_device(): lax.all_gather(doc_ids, 'kv', axis=0, tiled=True)]
    all_gather x1, waiting for transfers between devices: 24.7 us -> 35.2 us  [in_one_piece(): out = lax.all_gather(both, axis, axis=dim, tiled=True)]
    all_to_all x0 -> x1, starting transfers between devices: none -> 10.3 us  [attach_ladders(): left_arr = all_to_all(n_now, shard_axis, 0, 0)]
  transfers between devices with their start and end apart: 2 -> 3, of which waited for: 2 -> 2; matrix products, arithmetic and copies ran while one was open for 3% -> 5% of each run, Pallas kernels for 0% -> 0%
where the time goes in v1:
time: 183 us; the launch traced here: 182 us
  waiting for transfers between devices  44.3 us (24%)
  between operations  43.1 us (24%)
  local copies, waits for them, and re-layouts  31.4 us (17%)
  loops' own time  20.9 us (11%)
  blocking collectives  17.6 us (10%)
  starting transfers between devices  10.4 us (6%)
  other arithmetic  8.66 us (5%)
  matrix products  5.49 us (3%)
    all_gather x1, waiting for transfers between devices, in_one_piece(): out = lax.all_gather(both, axis, axis=dim, tiled=True)  35.2 us
    another operation x1, loops' own time, on_device(): result, _ = lax.scan(one_block, (initial, empty_tail), stacked)  20.7 us
    unnamed x2, blocking collectives  15.3 us
    dynamic_slice x40, local copies, waits for them, and re-layouts, on_device(): result, _ = lax.scan(one_block, (initial, empty_tail), stacked)  14.7 us
    all_to_all x1, starting transfers between devices, attach_ladders(): left_arr = all_to_all(n_now, shard_axis, 0, 0)  10.3 us
    all_gather x1, waiting for transfers between devices, collected_alike(): lax.all_gather(a, axis)  8.97 us
    slice x8, local copies, waits for them, and re-layouts, one_block(): doc_block[0]  5.17 us
    eq x8, other arithmetic, tail_state(): live = doc_rows == target_doc  5.03 us
  transfers between devices with their start and end apart: 3, of which 2 were waited for; matrix products, arithmetic and copies ran while one was open for 5% of the time, Pallas kernels for 0%

profile of v1, /device:TPU:2, one launch (start us, length us, event | category | flops | bytes accessed | tf_op | source)
XLA Modules:
  0.0 181.8 jit_solution(3110608633256792767)
XLA Ops:
  6.5 1.7 pad_maximum_fusion
  8.3 1.2 stack.2
  9.5 10.3 %all-to-all-start = ((s32[8,1,128]{2,1,0:T(1,128)}), s32[8,1,128]{2,1,0:T(1,128)S(1)}, u32[]{:S(2)}, u32[]{:S(2)}) async-start(s32[8,1,128]{2,1,0:T(1,128)} %stack.2), calls=%async_computation | async-start | bytes 8192 | tf_op jit(solution)/shard_map/all_to_all | solution.py:143
  19.9 1.3 copy.45
  21.5 1.3 dynamic-slice
  23.5 35.2 %all-gather.6.cloned.1.call-done = bf16[1024,1024]{1,0:T(8,128)(2,1)} async-done(((bf16[128,1024]{1,0:T(8,128)(2,1)}), bf16[1024,1024]{1,0:T(8,128)(2,1)}) %all-gather.6.cloned.1.call-update) | async-done | bytes 2097168 | tf_op jit(solution)/shard_map/all_gather | solution.py:18
  58.8 2.6 %fusion.103 = (bf16[1024,512]{1,0:T(8,128)(2,1)S(1)}, bf16[1024,512]{1,0:T(8,128)(2,1)}) fusion(bf16[1024,1024]{1,0:T(8,128)(2,1)} %all-gather.6.cloned.1.call-done), kind=kLoop, calls=%fused_computation.128 | loop fusion | bytes 4194304 | tf_op jit(solution)/shard_map/split | solution.py:19
  61.6 49.0 %while.21 = (s32[]{:T(128)}, f32[4,4,128]{2,1,0:T(4,128)S(1)}, f32[4,4,128]{2,1,0:T(4,128)S(1)}, f32[4,4,128,128]{3,2,1,0:T(8,128)S(1)}, f32[4,128,128]{2,1,0:T(...) while((s32[]{:T(128)}, f32[4,4,128]{2,1,0:T(4,128)S(1)}, ...), condition=%wide.region_5.6_spmd.clone, body=%wide.region_0.5_spmd.clone.sunk | while | flops 154259840 | bytes 8067273 | solution.py:201
  62.9 0.9 constant_dynamic-slice_fusion.6
  64.1 1.5 conditional.3
  70.3 0.9 constant_dynamic-slice_fusion.6
  76.2 0.9 constant_dynamic-slice_fusion.6
  82.2 0.9 constant_dynamic-slice_fusion.6
  88.1 0.9 constant_dynamic-slice_fusion.6
  94.1 0.9 constant_dynamic-slice_fusion.6
  100.0 0.9 constant_dynamic-slice_fusion.6
  106.0 0.9 constant_dynamic-slice_fusion.6
  110.8 2.3 %all-gather.2 = f32[8,128,128]{2,1,0:T(8,128)S(1)} all-gather(f32[4,128,128]{2,1,0:T(8,128)S(1)} %get-tuple-element.130), channel_id=4, replica_groups=mesh['seq_0'=8,'seq_1'=2,'kv'=8,'dp'=4] {'seq_1'}, dimensions={0}, use_global_device_ids=true | all-gather | bytes 786432 | tf_op jit(solution)/shard_map/all_gather | solution.py:53
  113.1 1.8 all-reduce
  119.9 1.3 dynamic-slice.1
  124.9 13.5 %all-reduce.1 = s32[16]{0:T(128)S(1)} all-reduce(s32[16]{0:T(128)S(1)} %fusion.99), channel_id=3, replica_groups=mesh['seq_0'=8,'seq_1'=2,'kv'=8,'dp'=4] {'seq_0'}, use_global_device_ids=true, to_apply=%add.1 | all-reduce | flops 16 | bytes 128
  161.6 9.0 %all-gather.8.cloned.1.call-done = f32[8,4,128,128]{3,2,1,0:T(8,128)} async-done(((f32[1,4,128,128]{3,2,1,0:T(8,128)}), f32[8,4,128,128]{3,2,1,0:T(8,128)}) %all-gather.8.cloned.1.call-update) | async-done | bytes 2097168 | tf_op jit(solution)/shard_map/all_gather | solution.py:53
  170.5 2.6 %multiply_reduce_fusion = (f32[128,4,4]{0,2,1:T(4,128)S(1)}, f32[128,4,4,128]{0,3,2,1:T(8,128)S(1)}) fusion(bf16[128,4,4,128]{0,3,2,1:T(8,128)(2,1)S(1)} %bitcast.202, f32[8,4,128,128]{3,2,1,0:T(8,128)} %all-gather.8.cloned.1.call-done, f32[8,128,128]{2,1,0:T(8,128)S(1)} %all-gather.2, pred[]{:T(512)S(6)} %lt.43, pred[]{:T(512)S(6)} %and.43, pred[]{:T(512)S(6)} %gt.31, ...), kind=kOutput, calls=%fused_computation.31 | convolution fusion | flops 405993472 | bytes 4202654 | tf_op jit(solution)/shard_map/rgqd,gde->rgqe/dot_general | solution.py:213
  173.7 1.3 copy.52
  (116 shorter events, 24.7 us)
Async XLA Ops:
  6.5 52.2 %all-gather.6.cloned.1.call-start = ((), (), s32[]{:S(2)}) async-start(), calls=%async_computation.1 | async-start | bytes 2359296 | tf_op jit(solution)/shard_map/all_gather | solution.py:18
  9.5 51.9 %all-to-all-start = ((s32[8,1,128]{2,1,0:T(1,128)}), s32[8,1,128]{2,1,0:T(1,128)S(1)}, u32[]{:S(2)}, u32[]{:S(2)}) async-start(s32[8,1,128]{2,1,0:T(1,128)} %stack.2), calls=%async_computation | async-start | bytes 8192 | tf_op jit(solution)/shard_map/all_to_all | solution.py:143
  19.8 150.7 %all-gather.8.cloned.1.call-start = ((), (), s32[]{:S(2)}) async-start(), calls=%async_computation.2 | async-start | bytes 2359296 | tf_op jit(solution)/shard_map/all_gather | solution.py:53
  21.2 40.2 %copy-start = (bf16[128,2048]{0,1:T(8,128)(2,1)}, bf16[128,2048]{0,1:T(8,128)(2,1)S(1)}, u32[]{:S(2)}) copy-start(bf16[128,2048]{0,1:T(8,128)(2,1)S(1)} %copy.45) | copy-start | bytes 1572868
  23.5 38.0 %copy-start.2 = (s32[128]{0:T(128)S(1)}, s32[128]{0:T(128)}, u32[]{:S(2)}) copy-start(s32[128]{0:T(128)} %param.13) | copy-start | bytes 1540
  61.5 60.4 %copy-start.4 = (f32[16]{0:T(128)S(1)}, f32[16]{0:T(128)}, u32[]{:S(2)}) copy-start(f32[16]{0:T(128)} %param.14) | copy-start | bytes 196
  110.8 59.8 %copy-start.1 = (bf16[128,2048]{0,1:T(8,128)(2,1)S(1)}, bf16[128,2048]{0,1:T(8,128)(2,1)}, u32[]{:S(2)}) copy-start(bf16[128,2048]{0,1:T(8,128)(2,1)} %copy-done) | copy-start | bytes 1572868
  161.6 11.6 %copy-start.3 = (f32[2048]{0:T(1024)S(1)}, f32[2048]{0:T(1024)}, u32[]{:S(2)}) copy-start(f32[2048]{0:T(1024)} %param.15) | copy-start | bytes 24580
Sparse Core Ops, SparseCore 0:
  9.4 49.2 all-gather.5
  120.0 50.5 all-gather.7
